TPU v7x, 32 devices: a whole 2x2x4 slice. The times are simulated.
32 devices in a mesh: shard: 16 (over z, x, core), ctx: 2 (over y).
Axes of the slice: x: 2, y: 2, z: 4, core: 2. Of those that a mesh axis runs over, the one named last changes fastest.
Arguments:
- tokens: bfloat16 [8192, 576], P(('shard', 'ctx')), may hold values from -6 to 6
- cotangent: bfloat16 [8192, 576], P(('shard', 'ctx')), may hold values from -6 to 6
- seq_lengths: int32 [16], P('shard'), may hold values from 64 to 512, as said below
- attn_params: float32 [885888], P('shard')
- attn_first: float32 [885888], P('shard'), may hold values from -6 to 6
- attn_second: float32 [885888], P('shard'), may hold values from 1 to 100
- ffn_params: float32 [2654208], P('shard')
- ffn_first: float32 [2654208], P('shard'), may hold values from -6 to 6
- ffn_second: float32 [2654208], P('shard'), may hold values from 1 to 100
Outputs:
- outputs: bfloat16 [8192, 576], P(('shard', 'ctx'))
- grad_tokens: bfloat16 [8192, 576], P(('shard', 'ctx'))
- attn_grad: float32 [885888], P('shard')
- ffn_grad: float32 [2654208], P('shard')
- attn_new: float32 [885888], P('shard')
- attn_first_new: float32 [885888], P('shard')
- attn_second_new: float32 [885888], P('shard')
- ffn_new: float32 [2654208], P('shard')
- ffn_first_new: float32 [2654208], P('shard')
- ffn_second_new: float32 [2654208], P('shard')
Inputs may be any that keep to these rules, and one draw needn't show every extreme that they name: `seq_lengths`: in every draw some sequence fills all 512 slots.
All inputs are finite; a program needn't handle non-finite values.
Results may differ from a plain program's by a relative error of at most 0.01.
The roundings to bfloat16 on the way count: a program that leaves them out, or rounds other values in their place, can miss the bound.
Values may be sent and summed in bfloat16 or wider, within the bound.
A program may use at most 128 MiB of HBM per device.

v0:
```python
import math
import jax
import jax.numpy as jnp
from jax import lax
from jax.sharding import PartitionSpec as P

MODEL_WIDTH = 576
QUERY_HEADS = 9
KEY_VALUE_HEADS = 3
HEAD_SIZE = 64
FF = 1536
ADAM_STEP = 3
rms_eps = 1e-05
rope_base = 100000.0
beta_one = 0.9
beta_two = 0.95
learn_rate = 0.02
decay_rate = 0.1
adam_eps = 1e-08
masked_score = -1e30


def split_flattened(flattened, shapes):
    pieces = []
    offset = 0
    for shape in shapes:
        width = 1
        for extent in shape:
            width = width * extent
        pieces.append(flattened[offset : offset + width].reshape(shape))
        offset = offset + width
    return pieces


def split_attention(flattened):
    return split_flattened(
        flattened,
        (
            (MODEL_WIDTH, QUERY_HEADS * HEAD_SIZE),
            (MODEL_WIDTH, KEY_VALUE_HEADS * HEAD_SIZE),
            (MODEL_WIDTH, KEY_VALUE_HEADS * HEAD_SIZE),
            (QUERY_HEADS * HEAD_SIZE, MODEL_WIDTH),
            (MODEL_WIDTH,),
            (MODEL_WIDTH,),
        ),
    )


def split_feedforward(flattened):
    return split_flattened(flattened, ((MODEL_WIDTH, FF), (MODEL_WIDTH, FF), (FF, MODEL_WIDTH)))


def rope_tables(positions):
    index = jnp.arange(HEAD_SIZE // 2).astype(jnp.float32)
    inverse = jnp.exp(index * (-2.0 * math.log(rope_base) / HEAD_SIZE))
    angles = positions.astype(jnp.float32)[:, None] * inverse[None, :]
    angles = jnp.concatenate([angles, angles], axis=1)
    return (jnp.cos(angles), jnp.sin(angles))


def apply_rotation(values, cosine_table, sine_table):
    half = values.shape[-1] // 2
    turned = jnp.concatenate([-values[..., half:], values[..., :half]], axis=-1)
    return values * cosine_table[:, None, :] + turned * sine_table[:, None, :]


def reverse_rotation(grads, cosine_table, sine_table):
    half = grads.shape[-1] // 2
    weighted = grads * sine_table[:, None, :]
    turned = jnp.concatenate([weighted[..., half:], -weighted[..., :half]], axis=-1)
    return grads * cosine_table[:, None, :] + turned


def norm_rows(values, gain):
    mean_sq = jnp.mean(values * values, axis=-1, keepdims=True)
    inverse = lax.rsqrt(mean_sq + rms_eps)
    scaled = values * inverse
    return (scaled, inverse, (scaled * gain).astype(jnp.bfloat16))


def norm_back(grad_normed, scaled, inverse, gain):
    grad_scaled = grad_normed * gain
    grad_gain = jnp.sum(grad_normed * scaled, axis=0)
    inner = jnp.mean(grad_scaled * scaled, axis=-1, keepdims=True)
    return (inverse * (grad_scaled - scaled * inner), grad_gain)


def attend(query_rows, keys, values, mask):
    row_entries = query_rows.shape[0]
    scale = 1.0 / math.sqrt(HEAD_SIZE)
    grouped_heads = query_rows.reshape(
        row_entries, KEY_VALUE_HEADS, QUERY_HEADS // KEY_VALUE_HEADS, HEAD_SIZE
    )
    scores = (
        jnp.einsum("tkgd,skd->kgts", grouped_heads, keys, preferred_element_type=jnp.float32)
        * scale
    )
    scores = jnp.where(mask[None, None], scores, masked_score)
    top = jnp.max(scores, axis=-1, keepdims=True)
    total = jnp.sum(jnp.exp(scores - top), axis=-1, keepdims=True)
    log_total = top + jnp.log(total)
    probs = jnp.exp(scores - log_total).astype(jnp.bfloat16)
    mixture = jnp.einsum("kgts,skd->tkgd", probs, values, preferred_element_type=jnp.float32)
    return (mixture.reshape(row_entries, QUERY_HEADS * HEAD_SIZE).astype(jnp.bfloat16), log_total)


def attend_back(query_rows, keys, values, mask, log_total, mixture, mixture_gradient):
    row_entries = query_rows.shape[0]
    head_group = QUERY_HEADS // KEY_VALUE_HEADS
    scale = 1.0 / math.sqrt(HEAD_SIZE)
    grouped_queries = query_rows.reshape(
        row_entries, KEY_VALUE_HEADS, head_group, HEAD_SIZE
    ).transpose(1, 0, 2, 3)
    gradient_groups = mixture_gradient.reshape(
        row_entries, KEY_VALUE_HEADS, head_group, HEAD_SIZE
    ).transpose(1, 0, 2, 3)
    mixture_groups = mixture.reshape(row_entries, KEY_VALUE_HEADS, head_group, HEAD_SIZE).transpose(
        1, 0, 2, 3
    )
    key_groups = keys.transpose(1, 0, 2)
    value_groups = values.transpose(1, 0, 2)

    def one_group(item):
        query_one, key_one, value_one, total_one, mixed_one, grad_one = item
        scores = (
            jnp.einsum("tgd,sd->gts", query_one, key_one, preferred_element_type=jnp.float32)
            * scale
        )
        scores = jnp.where(mask[None], scores, masked_score)
        probs = jnp.exp(scores - total_one)
        delta = jnp.einsum("tgd,tgd->gt", grad_one, mixed_one, preferred_element_type=jnp.float32)
        grad_probs = jnp.einsum(
            "tgd,sd->gts", grad_one, value_one, preferred_element_type=jnp.float32
        )
        grad_scores = (probs * (grad_probs - delta[..., None]) * scale).astype(jnp.bfloat16)
        grad_query = jnp.einsum(
            "gts,sd->tgd", grad_scores, key_one, preferred_element_type=jnp.float32
        )
        key_gradient = jnp.einsum(
            "gts,tgd->sd", grad_scores, query_one, preferred_element_type=jnp.float32
        )
        value_gradient = jnp.einsum(
            "gts,tgd->sd", probs.astype(jnp.bfloat16), grad_one, preferred_element_type=jnp.float32
        )
        return (grad_query, key_gradient, value_gradient)

    grad_query, key_gradient, value_gradient = lax.map(
        one_group,
        (grouped_queries, key_groups, value_groups, log_total, mixture_groups, gradient_groups),
    )
    grad_query = grad_query.transpose(1, 0, 2, 3).reshape(row_entries, QUERY_HEADS, HEAD_SIZE)
    return (grad_query, key_gradient.transpose(1, 0, 2), value_gradient.transpose(1, 0, 2))


def adam_update(params, first, second, grads):
    first_new = beta_one * first + (1.0 - beta_one) * grads
    second_new = beta_two * second + (1.0 - beta_two) * grads * grads
    corr_one = 1.0 - beta_one**ADAM_STEP
    corr_two = 1.0 - beta_two**ADAM_STEP
    moved = first_new / corr_one / (jnp.sqrt(second_new / corr_two) + adam_eps)
    return (params - learn_rate * (moved + decay_rate * params), first_new, second_new)


def owner_layout(term, owners, pair):
    columns = term.shape[0] // owners
    padded_columns = columns + -columns % pair
    table = term.reshape(owners, columns)
    return (jnp.pad(table, ((0, 0), (0, padded_columns - columns))).reshape(-1), columns)


def body(
    tokens,
    cotangent,
    seq_lengths,
    attn_params,
    attn_first,
    attn_second,
    ffn_params,
    ffn_first,
    ffn_second,
):
    row_entries = tokens.shape[0]
    ctx_count = lax.axis_size("ctx")
    ctx_index = lax.axis_index("ctx")
    owners = lax.axis_size("shard")
    slot_entries = row_entries * ctx_count
    length = seq_lengths[0]
    low_params = (attn_params.astype(jnp.bfloat16), ffn_params.astype(jnp.bfloat16))
    attn_whole, ffn_whole = (
        lax.all_gather(low_params[0], "shard", axis=0, tiled=True),
        lax.all_gather(low_params[1], "shard", axis=0, tiled=True),
    )
    w_query, key_matrix, value_matrix, w_out, gain_one, gain_two = split_attention(attn_whole)
    w_gate, w_up, w_down = split_feedforward(ffn_whole)
    gain_one = gain_one.astype(jnp.float32)
    gain_two = gain_two.astype(jnp.float32)
    positions = ctx_index * row_entries + jnp.arange(row_entries)
    key_positions = jnp.arange(slot_entries)
    valid = (positions < length).astype(jnp.float32)[:, None]
    has_rows = ctx_index * row_entries < length
    mask = (key_positions[None, :] <= positions[:, None]) & (key_positions[None, :] < length)
    inputs = tokens.astype(jnp.float32)
    scaled_one, inv_one, first_normed = norm_rows(inputs, gain_one)
    query_raw = jnp.dot(first_normed, w_query, preferred_element_type=jnp.float32).reshape(
        row_entries, QUERY_HEADS, HEAD_SIZE
    )
    unrotated_key = jnp.dot(first_normed, key_matrix, preferred_element_type=jnp.float32).reshape(
        row_entries, KEY_VALUE_HEADS, HEAD_SIZE
    )
    value_reduced = jnp.dot(first_normed, value_matrix, preferred_element_type=jnp.float32).astype(
        jnp.bfloat16
    )
    cosine_table, sine_table = rope_tables(positions)
    query_low = apply_rotation(query_raw, cosine_table, sine_table).astype(jnp.bfloat16)
    key_reduced = (
        apply_rotation(unrotated_key, cosine_table, sine_table)
        .astype(jnp.bfloat16)
        .reshape(row_entries, KEY_VALUE_HEADS * HEAD_SIZE)
    )
    full_keys, full_values = (
        lax.all_gather(key_reduced, "ctx", axis=0, tiled=True),
        lax.all_gather(value_reduced, "ctx", axis=0, tiled=True),
    )
    full_keys = full_keys.reshape(slot_entries, KEY_VALUE_HEADS, HEAD_SIZE)
    full_values = full_values.reshape(slot_entries, KEY_VALUE_HEADS, HEAD_SIZE)
    mixture, log_total = lax.cond(
        has_rows,
        lambda: attend(query_low, full_keys, full_values, mask),
        lambda: (
            jnp.zeros((row_entries, QUERY_HEADS * HEAD_SIZE), jnp.bfloat16),
            jnp.zeros(
                (KEY_VALUE_HEADS, QUERY_HEADS // KEY_VALUE_HEADS, row_entries, 1), jnp.float32
            ),
        ),
    )
    hidden = inputs + jnp.dot(mixture, w_out, preferred_element_type=jnp.float32)
    scaled_two, inv_two, normed_two = norm_rows(hidden, gain_two)
    gate = jnp.dot(normed_two, w_gate, preferred_element_type=jnp.float32)
    upward = jnp.dot(normed_two, w_up, preferred_element_type=jnp.float32)
    sigma = jax.nn.sigmoid(gate)
    activ = (gate * sigma * upward).astype(jnp.bfloat16)
    result = hidden + jnp.dot(activ, w_down, preferred_element_type=jnp.float32)
    outputs = (valid * result).astype(jnp.bfloat16)
    grad_result = valid * cotangent.astype(jnp.float32)
    grad_low = grad_result.astype(jnp.bfloat16)
    grad_w_down = jnp.dot(activ.T, grad_low, preferred_element_type=jnp.float32)
    grad_activ = jnp.dot(grad_low, w_down.T, preferred_element_type=jnp.float32)
    grad_gate = (grad_activ * upward * sigma * (1.0 + gate * (1.0 - sigma))).astype(jnp.bfloat16)
    grad_upward = (grad_activ * gate * sigma).astype(jnp.bfloat16)
    grad_w_gate = jnp.dot(normed_two.T, grad_gate, preferred_element_type=jnp.float32)
    grad_w_up = jnp.dot(normed_two.T, grad_upward, preferred_element_type=jnp.float32)
    ffn_term = jnp.concatenate(
        [grad_w_gate.reshape(-1), grad_w_up.reshape(-1), grad_w_down.reshape(-1)]
    )
    ffn_padded, ffn_columns = owner_layout(ffn_term, owners, ctx_count)
    grad_normed_two = jnp.dot(grad_gate, w_gate.T, preferred_element_type=jnp.float32) + jnp.dot(
        grad_upward, w_up.T, preferred_element_type=jnp.float32
    )
    grad_hidden_part, grad_gain_two = norm_back(grad_normed_two, scaled_two, inv_two, gain_two)
    grad_hidden = grad_result + grad_hidden_part
    grad_hidden_low = grad_hidden.astype(jnp.bfloat16)
    grad_w_out = jnp.dot(mixture.T, grad_hidden_low, preferred_element_type=jnp.float32)
    mixture_gradient = jnp.dot(grad_hidden_low, w_out.T, preferred_element_type=jnp.float32).astype(
        jnp.bfloat16
    )
    grad_query, full_key_gradient, full_value_gradient = lax.cond(
        has_rows,
        lambda: attend_back(
            query_low, full_keys, full_values, mask, log_total, mixture, mixture_gradient
        ),
        lambda: (
            jnp.zeros((row_entries, QUERY_HEADS, HEAD_SIZE), jnp.float32),
            jnp.zeros((slot_entries, KEY_VALUE_HEADS, HEAD_SIZE), jnp.float32),
            jnp.zeros((slot_entries, KEY_VALUE_HEADS, HEAD_SIZE), jnp.float32),
        ),
    )
    key_gradient, value_gradient = (
        lax.psum_scatter(
            full_key_gradient.reshape(slot_entries, KEY_VALUE_HEADS * HEAD_SIZE),
            "ctx",
            scatter_dimension=0,
            tiled=True,
        ),
        lax.psum_scatter(
            full_value_gradient.reshape(slot_entries, KEY_VALUE_HEADS * HEAD_SIZE),
            "ctx",
            scatter_dimension=0,
            tiled=True,
        ),
    )
    grad_query_raw = (
        reverse_rotation(grad_query, cosine_table, sine_table)
        .astype(jnp.bfloat16)
        .reshape(row_entries, QUERY_HEADS * HEAD_SIZE)
    )
    unrotated_key_gradient = (
        reverse_rotation(
            key_gradient.reshape(row_entries, KEY_VALUE_HEADS, HEAD_SIZE), cosine_table, sine_table
        )
        .astype(jnp.bfloat16)
        .reshape(row_entries, KEY_VALUE_HEADS * HEAD_SIZE)
    )
    plain_value_gradient = value_gradient.astype(jnp.bfloat16)
    grad_w_query = jnp.dot(first_normed.T, grad_query_raw, preferred_element_type=jnp.float32)
    grad_w_key = jnp.dot(first_normed.T, unrotated_key_gradient, preferred_element_type=jnp.float32)
    grad_w_value = jnp.dot(first_normed.T, plain_value_gradient, preferred_element_type=jnp.float32)
    grad_normed_one = jnp.dot(grad_query_raw, w_query.T, preferred_element_type=jnp.float32)
    grad_normed_one = grad_normed_one + jnp.dot(
        unrotated_key_gradient, key_matrix.T, preferred_element_type=jnp.float32
    )
    grad_normed_one = grad_normed_one + jnp.dot(
        plain_value_gradient, value_matrix.T, preferred_element_type=jnp.float32
    )
    grad_input_part, grad_gain_one = norm_back(grad_normed_one, scaled_one, inv_one, gain_one)
    grad_tokens = (grad_hidden + grad_input_part).astype(jnp.bfloat16)
    attn_term = jnp.concatenate(
        [
            grad_w_query.reshape(-1),
            grad_w_key.reshape(-1),
            grad_w_value.reshape(-1),
            grad_w_out.reshape(-1),
            grad_gain_one,
            grad_gain_two,
        ]
    )
    attn_padded, attn_columns = owner_layout(attn_term, owners, ctx_count)
    attn_half, ffn_half = (
        lax.psum_scatter(attn_padded, ("shard", "ctx"), scatter_dimension=0, tiled=True),
        lax.psum_scatter(ffn_padded, ("shard", "ctx"), scatter_dimension=0, tiled=True),
    )
    attn_joined, ffn_joined = (
        lax.all_gather(attn_half, "ctx", axis=0, tiled=True),
        lax.all_gather(ffn_half, "ctx", axis=0, tiled=True),
    )
    attn_grad = attn_joined[:attn_columns]
    attn_new, attn_first_new, attn_second_new = adam_update(
        attn_params, attn_first, attn_second, attn_grad
    )
    ffn_new, ffn_first_new, ffn_second_new = adam_update(
        ffn_params, ffn_first, ffn_second, ffn_joined
    )
    return (
        outputs,
        grad_tokens,
        attn_grad,
        ffn_joined,
        attn_new,
        attn_first_new,
        attn_second_new,
        ffn_new,
        ffn_first_new,
        ffn_second_new,
    )


def solution(mesh):
    return jax.shard_map(
        body,
        mesh=mesh,
        in_specs=(
            P(("shard", "ctx"), None),
            P(("shard", "ctx"), None),
            P("shard"),
            P("shard"),
            P("shard"),
            P("shard"),
            P("shard"),
            P("shard"),
            P("shard"),
        ),
        out_specs=(
            P(("shard", "ctx"), None),
            P(("shard", "ctx"), None),
            P("shard"),
            P("shard"),
            P("shard"),
            P("shard"),
            P("shard"),
            P("shard"),
            P("shard"),
            P("shard"),
        ),
        check_vma=False,
    )
```

profile of v0, /device:TPU:0, one launch (start us, length us, event | category | flops | bytes accessed | tf_op | source)
XLA Modules:
  0.0 597.9 jit_solution(964759938562371816)
XLA Ops:
  16.1 95.9 %all-reduce.9.cloned.1.call-done = bf16[885888]{0:T(1024)(128)(2,1)} async-done(((bf16[885888]{0:T(1024)(128)(2,1)}), bf16[885888]{0:T(1024)(128)(2,1)}) %all-reduce.9.cloned.1.call-update) | async-done | bytes 1771792
  119.5 5.3 all_gather.19
  125.2 5.3 all_gather.20
  131.9 4.6 conditional.2
  134.5 2.0 fusion.3
  137.3 33.6 %all-gather.2.cloned.1.call-done = bf16[2654208]{0:T(1024)(128)(2,1)} async-done(((bf16[165888]{0:T(1024)(128)(2,1)}), bf16[2654208]{0:T(1024)(128)(2,1)}) %all-gather.2.cloned.1.call-update) | async-done | bytes 5308432 | tf_op jit(solution)/shard_map/all_gather | solution.py:191
  170.9 4.7 fusion.88
  175.6 3.0 slice.124
  178.6 3.6 slice.126
  182.1 3.4 fusion.93
  185.6 2.0 fusion.94
  187.5 4.3 slice.128
  191.9 4.8 multiply_convert_fusion
  201.8 27.9 %conditional.3 = (f32[256,9,64]{0,2,1:T(8,128)}, f32[512,3,64]{0,2,1:T(8,128)}, f32[512,3,64]{0,2,1:T(8,128)}) conditional(s32[]{:T(128)} %convert_element_type.112, () %tuple.30, (bf16[256,9,64]{0,2,1:T(8,128)(2,1)S(1)}, bf16[512,3,64]{0,2,1:T(8,128)(2,1)}, bf16[512,3,64]{0,2,1:T(8,128)(2,1)}, bf16[256,576]{0,1:T(8,128)(2,1)S(1)}, ...), branch_computations={%region_7.8_spmd, %region_8.0_spmd} | conditional | flops 254999808 | bytes 16739761 | solution.py:266
  201.8 27.9 %while.13 = (s32[]{:T(128)}, f32[3,256,3,64]{1,3,2,0:T(8,128)}, f32[3,512,64]{1,2,0:T(8,128)}, f32[3,512,64]{1,2,0:T(8,128)}, bf16[3,512,64]{1,2,0:T(8,128)(2,1)...) while((s32[]{:T(128)}, f32[3,256,3,64]{1,3,2,0:T(8,128)}, ...), condition=%wide.region_10.10_spmd, body=%wide.region_9.9_spmd.sunk | while | flops 254999808 | bytes 16739633 | solution.py:147
  231.2 2.7 fusion.61
  238.0 1.9 reshape.296
  239.9 5.4 reshape.299
  245.3 2.4 fusion.97
  247.6 4.6 reshape.298
  252.3 2.4 fusion.96
  254.7 4.6 reshape.297
  259.3 11.2 %pad_maximum_fusion = f32[2654208]{0:T(1024)} fusion(f32[884736]{0:T(1024)} %reshape.299, f32[884736]{0:T(1024)} %reshape.298, f32[884736]{0:T(1024)} %reshape.297), kind=kLoop, calls=%fused_computation.50 | loop fusion | flops 5308416 | bytes 21233664 | tf_op jit(solution)/shard_map/concatenate | solution.py:252
  274.4 2.1 reshape.294
  278.9 2.0 fusion.74
  280.9 2.3 reshape.295
  283.2 2.9 fusion.50
  286.1 25.4 %concatenate.37 = f32[885888]{0:T(1024)} concatenate(f32[331776]{0:T(1024)S(1)} %copy-done.16, f32[110592]{0:T(1024)} %reshape.294, f32[110592]{0:T(1024)} %reshape.295, f32[331776]{0:T(1024)S(1)} %reshape.296, f32[576]{0:T(1024)S(1)} %get-tuple-element.157, f32[576]{0:T(1024)S(1)} %copy-done.48), dimensions={0} | concatenate | bytes 7087104 | tf_op jit(solution)/shard_map/concatenate | solution.py:316
  313.4 2.8 fusion.38
  317.2 242.8 %all-reduce.13.cloned.1.call-done = (f32[885888]{0:T(1024)}, f32[2654208]{0:T(1024)}) async-done(((f32[885888]{0:T(1024)}, f32[2654208]{0:T(1024)}), (f32[885888]{0:T(1024)}, f32[2654208]{0:T(1024)})) %all-reduce.13.cloned.1.call-update) | async-done | bytes 14160400
  563.3 12.8 %all_gather.23 = f32[165888]{0:T(1024)S(1)} all-gather(f32[82944]{0:T(1024)S(1)} %dynamic-slice.3), channel_id=1, replica_groups=mesh['shard'=16,'ctx'=2] {'ctx'}, dimensions={0}, use_global_device_ids=true | all-gather | bytes 995328 | tf_op jit(solution)/shard_map/all_gather | solution.py:333
  577.7 8.9 %all-reduce.11.cloned.1.call-done = f32[55368]{0:T(1024)} async-done(((f32[55368]{0:T(1024)}), f32[55368]{0:T(1024)}) %all-reduce.11.cloned.1.call-update) | async-done | bytes 221488
  (250 shorter events, 75.5 us)
Async XLA Ops:
  7.2 104.9 %all-reduce.9.cloned.1.call-start = ((), (), s32[]{:S(2)}) async-start(), calls=%async_computation.5 | async-start | bytes 3547136
  12.7 158.1 %all-gather.2.cloned.1.call-start = ((), (), s32[]{:S(2)}) async-start(), calls=%async_computation.2 | async-start | bytes 5640192 | tf_op jit(solution)/shard_map/all_gather | solution.py:191
  13.6 257.0 %reduce-scatter.3.cloned.1.call-start = ((), (), s32[]{:S(2)}) async-start(), calls=%async_computation.3 | async-start | bytes 589824 | tf_op jit(solution)/shard_map/reduce_scatter | solution.py:278
  14.7 116.4 %copy-start.32 = (f32[256,64]{0,1:T(8,128)}, f32[256,64]{0,1:T(8,128)S(1)}, u32[]{:S(2)}) copy-start(f32[256,64]{0,1:T(8,128)S(1)} %get-tuple-element.211) | copy-start | bytes 196612
  14.7 116.4 %copy-start.34 = (f32[256,64]{0,1:T(8,128)}, f32[256,64]{0,1:T(8,128)S(1)}, u32[]{:S(2)}) copy-start(f32[256,64]{0,1:T(8,128)S(1)} %get-tuple-element.212) | copy-start | bytes 196612
  116.7 8.1 %copy-start.38 = (bf16[576,192]{1,0:T(8,128)(2,1)}, bf16[576,192]{1,0:T(8,128)(2,1)S(1)}, u32[]{:S(2)}) copy-start(bf16[576,192]{1,0:T(8,128)(2,1)S(1)} %reshape.286) | copy-start | bytes 663556
  117.3 19.3 %copy-start.10 = (bf16[576,576]{1,0:T(8,128)(2,1)}, bf16[576,576]{1,0:T(8,128)(2,1)S(1)}, u32[]{:S(2)}) copy-start(bf16[576,576]{1,0:T(8,128)(2,1)S(1)} %reshape.288) | copy-start | bytes 1990660
  124.8 7.1 %copy-start.30 = (bf16[512,192]{0,1:T(8,128)(2,1)}, bf16[512,192]{0,1:T(8,128)(2,1)S(1)}, u32[]{:S(2)}) copy-start(bf16[512,192]{0,1:T(8,128)(2,1)S(1)} %all_gather.19) | copy-start | bytes 589828
  137.2 48.3 %copy-start.7 = (bf16[256,576]{0,1:T(8,128)(2,1)}, bf16[256,576]{0,1:T(8,128)(2,1)S(1)}, u32[]{:S(2)}) copy-start(bf16[256,576]{0,1:T(8,128)(2,1)S(1)} %multiply_convert_fusion.3) | copy-start | bytes 884740
  187.5 4.3 copy-start.39
  191.9 4.8 copy-start.1
  205.8 4.3 copy-start.3
  215.1 4.3 copy-start.3
  224.4 4.3 copy-start.3
  229.7 49.2 %reduce-scatter.5.cloned.1.call-start = ((), (), s32[]{:S(2)}) async-start(), calls=%async_computation.4 | async-start | bytes 589824 | tf_op jit(solution)/shard_map/reduce_scatter | solution.py:284
  239.9 5.4 copy-start.8
  239.9 5.4 copy-start.20
  247.6 4.7 copy-start.22
  259.3 11.3 %copy-start.35 = (f32[256,64]{0,1:T(8,128)S(1)}, f32[256,64]{0,1:T(8,128)}, u32[]{:S(2)}) copy-start(f32[256,64]{0,1:T(8,128)} %copy-done.34) | copy-start | bytes 196612
  259.3 300.8 %all-reduce.13.cloned.1.call-start = ((), (), s32[]{:S(2)}) async-start(), calls=%async_computation.7 | async-start | bytes 28327936
  271.5 5.0 copy-start.29
  271.6 6.1 %copy-start.13 = (bf16[576,576]{1,0:T(8,128)(2,1)S(1)}, bf16[576,576]{1,0:T(8,128)(2,1)}, u32[]{:S(2)}) copy-start(bf16[576,576]{1,0:T(8,128)(2,1)} %copy-done.12) | copy-start | bytes 1990660
  271.6 6.1 %copy-start.25 = (bf16[256,9,64]{0,2,1:T(8,128)(2,1)S(1)}, bf16[256,9,64]{0,2,1:T(8,128)(2,1)}, u32[]{:S(2)}) copy-start(bf16[256,9,64]{0,2,1:T(8,128)(2,1)} %copy-done.24) | copy-start | bytes 884740
  280.9 5.2 copy-start.16
  280.9 5.2 copy-start.48
  311.5 275.1 %all-reduce.11.cloned.1.call-start = ((), (), s32[]{:S(2)}) async-start(), calls=%async_computation.6 | async-start | bytes 450560
  316.3 259.8 %copy-start.27 = (f32[165888]{0:T(1024)S(1)}, f32[165888]{0:T(1024)}, u32[]{:S(2)}) copy-start(f32[165888]{0:T(1024)} %param.21) | copy-start | bytes 1990660
  316.3 259.8 %copy-start.44 = (f32[165888]{0:T(1024)S(1)}, f32[165888]{0:T(1024)}, u32[]{:S(2)}) copy-start(f32[165888]{0:T(1024)} %param.22) | copy-start | bytes 1990660
  316.3 259.7 %copy-start.45 = (f32[165888]{0:T(1024)S(1)}, f32[165888]{0:T(1024)}, u32[]{:S(2)}) copy-start(f32[165888]{0:T(1024)} %param.23) | copy-start | bytes 1990660
  576.1 10.6 %copy-start.41 = (f32[55368]{0:T(1024)S(1)}, f32[55368]{0:T(1024)}, u32[]{:S(2)}) copy-start(f32[55368]{0:T(1024)} %param.18) | copy-start | bytes 664420
  576.1 10.6 %copy-start.46 = (f32[55368]{0:T(1024)S(1)}, f32[55368]{0:T(1024)}, u32[]{:S(2)}) copy-start(f32[55368]{0:T(1024)} %param.19) | copy-start | bytes 664420
  576.1 10.6 %copy-start.47 = (f32[55368]{0:T(1024)S(1)}, f32[55368]{0:T(1024)}, u32[]{:S(2)}) copy-start(f32[55368]{0:T(1024)} %param.20) | copy-start | bytes 664420
  (40 other events, 89.9 us)
Sparse Core Ops, SparseCore 0:
  12.9 99.1 all-reduce.8
  114.8 56.0 all-gather.1
  229.8 11.7 reduce-scatter.2
  259.4 11.7 reduce-scatter.4
  311.7 248.3 all-reduce.12
  562.8 23.7 all-reduce.10
where the time goes:
time: 600 us; the launch traced here: 598 us
  waiting for transfers between devices  381 us (64%)
  local copies, waits for them, and re-layouts  88.9 us (15%)
  matrix products  58.9 us (10%)
  other arithmetic  27.6 us (5%)
  blocking collectives  23.4 us (4%)
  between operations  16.8 us (3%)
    unnamed x9, waiting for transfers between devices  348 us
    all_gather x1, waiting for transfers between devices, body(): lax.all_gather(low_params[1], 'shard', axis=0, tiled=True)  33.6 us
    concatenate x1, local copies, waits for them, and re-layouts, body(): jnp.concatenate([grad_w_query.reshape(-1), grad_w_key.reshape(-1), grad_w...  25.4 us
    slice x6, local copies, waits for them, and re-layouts, split_flattened(): pieces.append(flattened[offset:offset + width].reshape(shape))  18 us
    unnamed x105, local copies, waits for them, and re-layouts  13.8 us
    all_gather x1, blocking collectives, body(): lax.all_gather(ffn_half, 'ctx', axis=0, tiled=True)  12.8 us
  transfers between devices with their start and end apart: 6, of which 4 were waited for; matrix products, arithmetic and copies ran while one was open for 12% of the time, Pallas kernels for 0%

commit v1 on v0

--- a/solution.py
+++ b/solution.py
@@ -18,6 +18,19 @@
 decay_rate = 0.1
 adam_eps = 1e-08
 masked_score = -1e30
+
+
+def gather_around(x, axis, dim):
+    devices, index, rows = (lax.axis_size(axis), lax.axis_index(axis), x.shape[dim])
+    upward = [(i, (i + 1) % devices) for i in range(devices)]
+    out = jnp.zeros((*x.shape[:dim], devices * rows, *x.shape[dim + 1 :]), x.dtype)
+    current = x
+    for step in range(devices):
+        source = (index - step) % devices
+        out = lax.dynamic_update_slice_in_dim(out, current, source * rows, axis=dim)
+        if step < devices - 1:
+            current = lax.ppermute(current, axis, upward)
+    return out
 
 
 def split_flattened(flattened, shapes):
@@ -188,7 +201,7 @@
     low_params = (attn_params.astype(jnp.bfloat16), ffn_params.astype(jnp.bfloat16))
     attn_whole, ffn_whole = (
         lax.all_gather(low_params[0], "shard", axis=0, tiled=True),
-        lax.all_gather(low_params[1], "shard", axis=0, tiled=True),
+        gather_around(low_params[1], "shard", 0),
     )
     w_query, key_matrix, value_matrix, w_out, gain_one, gain_two = split_attention(attn_whole)
     w_gate, w_up, w_down = split_feedforward(ffn_whole)

time: 600 us -> 725 us (1.21); the launches traced: 598 us -> 714 us
  local copies, waits for them, and re-layouts: 88.9 us -> 186 us
  waiting for transfers between devices: 381 us -> 402 us
    ppermute x0 -> x15, waiting for transfers between devices: none -> 97.4 us  [gather_around(): current = lax.ppermute(current, axis, upward)]
    dynamic_update_slice x0 -> x15, local copies, waits for them, and re-layouts: none -> 92.5 us  [gather_around(): out = lax.dynamic_update_slice_in_dim(out, current, source * rows, axis=dim)]
    unnamed x9 -> x8, waiting for transfers between devices: 348 us -> 304 us
    all_gather x1 -> x0, waiting for transfers between devices: 33.6 us -> none  [body(): lax.all_gather(low_params[1], 'shard', axis=0, tiled=True)]
  transfers between devices with their start and end apart: 6 -> 20, of which waited for: 4 -> 14; matrix products, arithmetic and copies ran while one was open for 12% -> 22% of each run, Pallas kernels for 0% -> 0%
where the time goes in v1:
time: 725 us; the launch traced here: 714 us
  waiting for transfers between devices  402 us (55%)
  local copies, waits for them, and re-layouts  186 us (26%)
  matrix products  57.5 us (8%)
  other arithmetic  27.2 us (4%)
  blocking collectives  23.6 us (3%)
  between operations  17 us (2%)
    unnamed x8, waiting for transfers between devices  304 us
    ppermute x15, waiting for transfers between devices, gather_around(): current = lax.ppermute(current, axis, upward)  97.4 us
    dynamic_update_slice x15, local copies, waits for them, and re-layouts, gather_around(): out = lax.dynamic_update_slice_in_dim(out, current, source * rows, axis=dim)  92.5 us
    concatenate x1, local copies, waits for them, and re-layouts, body(): jnp.concatenate([grad_w_query.reshape(-1), grad_w_key.reshape(-1), grad_w...  26 us
    slice x6, local copies, waits for them, and re-layouts, split_flattened(): pieces.append(flattened[offset:offset + width].reshape(shape))  20.1 us
  transfers between devices with their start and end apart: 20, of which 14 were waited for; matrix products, arithmetic and copies ran while one was open for 22% of the time, Pallas kernels for 0%

profile of v1, /device:TPU:0, one launch (start us, length us, event | category | flops | bytes accessed | tf_op | source)
XLA Modules:
  0.0 714.2 jit_solution(2308748482732726075)
XLA Ops:
  11.3 9.8 %collective-permute-done = bf16[165888]{0:T(1024)(128)(2,1)S(1)} collective-permute-done((bf16[165888]{0:T(1024)(128)(2,1)S(1)}, bf16[165888]{0:T(1024)(128)(2,1)S(1)}, u32[]{:S(2)}, u32[]{:S(2)}) %collective-permute-start) | collective-permute-done | bytes 331808 | tf_op jit(solution)/shard_map/ppermute | solution.py:32
  21.0 9.2 %collective-permute-done.1 = bf16[165888]{0:T(1024)(128)(2,1)S(1)} collective-permute-done((bf16[165888]{0:T(1024)(128)(2,1)S(1)}, bf16[165888]{0:T(1024)(128)(2,1)S(1)}, u32[]{:S(2)}, u32[]{:S(2)}) %collective-permute-start.1) | collective-permute-done | bytes 331808 | tf_op jit(solution)/shard_map/ppermute | solution.py:32
  39.6 12.7 %collective-permute-done.3 = bf16[165888]{0:T(1024)(128)(2,1)S(1)} collective-permute-done((bf16[165888]{0:T(1024)(128)(2,1)S(1)}, bf16[165888]{0:T(1024)(128)(2,1)S(1)}, u32[]{:S(2)}, u32[]{:S(2)}) %collective-permute-start.3) | collective-permute-done | bytes 331808 | tf_op jit(solution)/shard_map/ppermute | solution.py:32
  52.6 12.5 %collective-permute-done.4 = bf16[165888]{0:T(1024)(128)(2,1)S(1)} collective-permute-done((bf16[165888]{0:T(1024)(128)(2,1)S(1)}, bf16[165888]{0:T(1024)(128)(2,1)S(1)}, u32[]{:S(2)}, u32[]{:S(2)}) %collective-permute-start.4) | collective-permute-done | bytes 331808 | tf_op jit(solution)/shard_map/ppermute | solution.py:32
  65.1 9.2 %collective-permute-done.5 = bf16[165888]{0:T(1024)(128)(2,1)S(1)} collective-permute-done((bf16[165888]{0:T(1024)(128)(2,1)S(1)}, bf16[165888]{0:T(1024)(128)(2,1)S(1)}, u32[]{:S(2)}, u32[]{:S(2)}) %collective-permute-start.5) | collective-permute-done | bytes 331808 | tf_op jit(solution)/shard_map/ppermute | solution.py:32
  80.6 6.1 dynamic_update_slice.61
  86.7 49.7 %all-reduce.9.cloned.1.call-done = bf16[885888]{0:T(1024)(128)(2,1)} async-done(((bf16[885888]{0:T(1024)(128)(2,1)}), bf16[885888]{0:T(1024)(128)(2,1)}) %all-reduce.9.cloned.1.call-update) | async-done | bytes 1771792
  139.0 8.2 %collective-permute-done.8 = bf16[165888]{0:T(1024)(128)(2,1)} collective-permute-done((bf16[165888]{0:T(1024)(128)(2,1)S(1)}, bf16[165888]{0:T(1024)(128)(2,1)}, u32[]{:S(2)}, u32[]{:S(2)}) %collective-permute-start.8) | collective-permute-done | bytes 331808 | tf_op jit(solution)/shard_map/ppermute | solution.py:32
  149.0 7.7 %collective-permute-done.9 = bf16[165888]{0:T(1024)(128)(2,1)} collective-permute-done((bf16[165888]{0:T(1024)(128)(2,1)}, bf16[165888]{0:T(1024)(128)(2,1)}, u32[]{:S(2)}, u32[]{:S(2)}) %collective-permute-start.9) | collective-permute-done | bytes 331808 | tf_op jit(solution)/shard_map/ppermute | solution.py:32
  159.2 7.1 collective-permute-done.10
  166.4 9.4 %collective-permute-done.11 = bf16[165888]{0:T(1024)(128)(2,1)S(1)} collective-permute-done((bf16[165888]{0:T(1024)(128)(2,1)}, bf16[165888]{0:T(1024)(128)(2,1)S(1)}, u32[]{:S(2)}, u32[]{:S(2)}) %collective-permute-start.11) | collective-permute-done | bytes 331808 | tf_op jit(solution)/shard_map/ppermute | solution.py:32
  177.7 7.4 %collective-permute-done.12 = bf16[165888]{0:T(1024)(128)(2,1)} collective-permute-done((bf16[165888]{0:T(1024)(128)(2,1)S(1)}, bf16[165888]{0:T(1024)(128)(2,1)}, u32[]{:S(2)}, u32[]{:S(2)}) %collective-permute-start.12) | collective-permute-done | bytes 331808 | tf_op jit(solution)/shard_map/ppermute | solution.py:32
  203.2 6.2 dynamic_update_slice.62
  209.4 6.1 dynamic_update_slice.63
  215.6 6.1 dynamic_update_slice.64
  221.7 6.1 dynamic_update_slice.65
  227.8 6.3 dynamic_update_slice.66
  234.1 6.1 dynamic_update_slice.67
  240.2 6.2 dynamic_update_slice.68
  246.5 6.2 dynamic_update_slice.69
  252.7 6.2 dynamic_update_slice.70
  258.9 6.1 dynamic_update_slice.71
  265.0 6.2 dynamic_update_slice.72
  271.2 6.2 dynamic_update_slice.73
  277.5 6.1 dynamic_update_slice.74
  312.4 30.6 %conditional.3 = (f32[256,9,64]{0,2,1:T(8,128)}, f32[512,3,64]{0,2,1:T(8,128)}, f32[512,3,64]{0,2,1:T(8,128)}) conditional(s32[]{:T(128)} %convert_element_type.112, () %tuple.30, (bf16[256,9,64]{0,2,1:T(8,128)(2,1)}, bf16[512,3,64]{0,2,1:T(8,128)(2,1)}, bf16[512,3,64]{0,2,1:T(8,128)(2,1)}, bf16[256,576]{0,1:T(8,128)(2,1)S(1)}, ...), branch_computations={%region_7.8_spmd, %region_8.11_spmd} | conditional | flops 254999808 | bytes 14379385 | solution.py:279
  312.4 30.6 %while.13 = (s32[]{:T(128)}, f32[3,256,3,64]{1,3,2,0:T(8,128)}, f32[3,512,64]{1,2,0:T(8,128)}, f32[3,512,64]{1,2,0:T(8,128)}, bf16[3,512,64]{1,2,0:T(8,128)(2,1)...) while((s32[]{:T(128)}, f32[3,256,3,64]{1,3,2,0:T(8,128)}, ...), condition=%wide.region_10.10_spmd, body=%wide.region_9.9_spmd.sunk | while | flops 254999808 | bytes 14379257 | solution.py:160
  372.7 11.2 %pad_maximum_fusion = f32[2654208]{0:T(1024)} fusion(f32[884736]{0:T(1024)} %reshape.299, f32[884736]{0:T(1024)} %reshape.298, f32[884736]{0:T(1024)} %reshape.297), kind=kLoop, calls=%fused_computation.50 | loop fusion | flops 5308416 | bytes 21233664 | tf_op jit(solution)/shard_map/concatenate | solution.py:265
  399.5 26.0 %concatenate.37 = f32[885888]{0:T(1024)} concatenate(f32[331776]{0:T(1024)S(1)} %copy-done.16, f32[110592]{0:T(1024)} %reshape.294, f32[110592]{0:T(1024)} %reshape.295, f32[331776]{0:T(1024)S(1)} %reshape.296, f32[576]{0:T(1024)} %get-tuple-element.157, f32[576]{0:T(1024)S(1)} %get-tuple-element.155), dimensions={0} | concatenate | bytes 7087104 | tf_op jit(solution)/shard_map/concatenate | solution.py:329
  431.3 245.5 %all-reduce.13.cloned.1.call-done = (f32[885888]{0:T(1024)}, f32[2654208]{0:T(1024)}) async-done(((f32[885888]{0:T(1024)}, f32[2654208]{0:T(1024)}), (f32[885888]{0:T(1024)}, f32[2654208]{0:T(1024)})) %all-reduce.13.cloned.1.call-update) | async-done | bytes 14160400
  679.9 12.8 %all_gather.19 = f32[165888]{0:T(1024)S(1)} all-gather(f32[82944]{0:T(1024)S(1)} %dynamic-slice.3), channel_id=1, replica_groups=mesh['shard'=16,'ctx'=2] {'ctx'}, dimensions={0}, use_global_device_ids=true | all-gather | bytes 995328 | tf_op jit(solution)/shard_map/all_gather | solution.py:346
  694.4 8.9 %all-reduce.11.cloned.1.call-done = f32[55368]{0:T(1024)} async-done(((f32[55368]{0:T(1024)}), f32[55368]{0:T(1024)}) %all-reduce.11.cloned.1.call-update) | async-done | bytes 221488
  (309 shorter events, 169.1 us)
Async XLA Ops:
  7.2 129.2 %all-reduce.9.cloned.1.call-start = ((), (), s32[]{:S(2)}) async-start(), calls=%async_computation.4 | async-start | bytes 3547136
  10.8 10.2 %collective-permute-start = (bf16[165888]{0:T(1024)(128)(2,1)S(1)}, bf16[165888]{0:T(1024)(128)(2,1)S(1)}, u32[]{:S(2)}, u32[]{:S(2)}) collective-permute-start(bf16[165888]{0:T(1024)(128)(2,1)S(1)} %get-tuple-element.190), channel_id=1, source_target_pairs={{0,2},{2,4},{4,6},{6,8},{8,10},{10,12},{12,14},{14,16},{16,18},{18... | collective-permute-start | bytes 995336 | tf_op jit(solution)/shard_map/ppermute | solution.py:32
  21.0 9.2 %collective-permute-start.1 = (bf16[165888]{0:T(1024)(128)(2,1)S(1)}, bf16[165888]{0:T(1024)(128)(2,1)S(1)}, u32[]{:S(2)}, u32[]{:S(2)}) collective-permute-start(bf16[165888]{0:T(1024)(128)(2,1)S(1)} %collective-permute-done), channel_id=1, source_target_pairs={{0,2},{2,4},{4,6},{6,8},{8,10},{10,12},{12,14},{14,16},{16,18},{18... | collective-permute-start | bytes 995336 | tf_op jit(solution)/shard_map/ppermute | solution.py:32
  30.3 9.2 %collective-permute-start.2 = (bf16[165888]{0:T(1024)(128)(2,1)S(1)}, bf16[165888]{0:T(1024)(128)(2,1)S(1)}, u32[]{:S(2)}, u32[]{:S(2)}) collective-permute-start(bf16[165888]{0:T(1024)(128)(2,1)S(1)} %collective-permute-done.1), channel_id=1, source_target_pairs={{0,2},{2,4},{4,6},{6,8},{8,10},{10,12},{12,14},{14,16},{16,18},{18... | collective-permute-start | bytes 995336 | tf_op jit(solution)/shard_map/ppermute | solution.py:32
  34.2 349.7 %reduce-scatter.3.cloned.1.call-start = ((), (), s32[]{:S(2)}) async-start(), calls=%async_computation.2 | async-start | bytes 589824 | tf_op jit(solution)/shard_map/reduce_scatter | solution.py:291
  34.2 46.3 %copy-start.49 = (bf16[165888]{0:T(1024)(128)(2,1)S(1)}, bf16[165888]{0:T(1024)(128)(2,1)}, u32[]{:S(2)}) copy-start(bf16[165888]{0:T(1024)(128)(2,1)} %copy-done.48) | copy-start | bytes 995332
  39.5 12.8 %collective-permute-start.3 = (bf16[165888]{0:T(1024)(128)(2,1)S(1)}, bf16[165888]{0:T(1024)(128)(2,1)S(1)}, u32[]{:S(2)}, u32[]{:S(2)}) collective-permute-start(bf16[165888]{0:T(1024)(128)(2,1)S(1)} %collective-permute-done.2), channel_id=1, source_target_pairs={{0,2},{2,4},{4,6},{6,8},{8,10},{10,12},{12,14},{14,16},{16,18},{18... | collective-permute-start | bytes 995336 | tf_op jit(solution)/shard_map/ppermute | solution.py:32
  52.3 12.8 %collective-permute-start.4 = (bf16[165888]{0:T(1024)(128)(2,1)S(1)}, bf16[165888]{0:T(1024)(128)(2,1)S(1)}, u32[]{:S(2)}, u32[]{:S(2)}) collective-permute-start(bf16[165888]{0:T(1024)(128)(2,1)S(1)} %collective-permute-done.3), channel_id=1, source_target_pairs={{0,2},{2,4},{4,6},{6,8},{8,10},{10,12},{12,14},{14,16},{16,18},{18... | collective-permute-start | bytes 995336 | tf_op jit(solution)/shard_map/ppermute | solution.py:32
  52.4 124.4 %copy-start.34 = (f32[256,64]{0,1:T(8,128)}, f32[256,64]{0,1:T(8,128)S(1)}, u32[]{:S(2)}) copy-start(f32[256,64]{0,1:T(8,128)S(1)} %get-tuple-element.214) | copy-start | bytes 196612
  52.5 294.9 %copy-start.33 = (f32[256,64]{0,1:T(8,128)}, f32[256,64]{0,1:T(8,128)S(1)}, u32[]{:S(2)}) copy-start(f32[256,64]{0,1:T(8,128)S(1)} %get-tuple-element.213) | copy-start | bytes 196612
  65.1 72.7 %copy-start.52 = (bf16[165888]{0:T(1024)(128)(2,1)}, bf16[165888]{0:T(1024)(128)(2,1)S(1)}, u32[]{:S(2)}) copy-start(bf16[165888]{0:T(1024)(128)(2,1)S(1)} %collective-permute-done.4) | copy-start | bytes 995332
  65.1 9.2 %collective-permute-start.5 = (bf16[165888]{0:T(1024)(128)(2,1)S(1)}, bf16[165888]{0:T(1024)(128)(2,1)S(1)}, u32[]{:S(2)}, u32[]{:S(2)}) collective-permute-start(bf16[165888]{0:T(1024)(128)(2,1)S(1)} %collective-permute-done.4), channel_id=1, source_target_pairs={{0,2},{2,4},{4,6},{6,8},{8,10},{10,12},{12,14},{14,16},{16,18},{18... | collective-permute-start | bytes 995336 | tf_op jit(solution)/shard_map/ppermute | solution.py:32
  74.3 12.4 %collective-permute-start.6 = (bf16[165888]{0:T(1024)(128)(2,1)S(1)}, bf16[165888]{0:T(1024)(128)(2,1)}, u32[]{:S(2)}, u32[]{:S(2)}) collective-permute-start(bf16[165888]{0:T(1024)(128)(2,1)S(1)} %collective-permute-done.5), channel_id=1, source_target_pairs={{0,2},{2,4},{4,6},{6,8},{8,10},{10,12},{12,14},{14,16},{16,18},{18... | collective-permute-start | bytes 995336 | tf_op jit(solution)/shard_map/ppermute | solution.py:32
  74.5 122.0 %copy-start.37 = (pred[256,512]{0,1:T(8,128)(4,1)}, pred[256,512]{0,1:T(8,128)(4,1)S(1)}, u32[]{:S(2)}) copy-start(pred[256,512]{0,1:T(8,128)(4,1)S(1)} %fusion.56) | copy-start | bytes 393220
  86.7 51.1 %collective-permute-start.7 = (bf16[165888]{0:T(1024)(128)(2,1)}, bf16[165888]{0:T(1024)(128)(2,1)S(1)}, u32[]{:S(2)}, u32[]{:S(2)}) collective-permute-start(bf16[165888]{0:T(1024)(128)(2,1)} %collective-permute-done.6), channel_id=1, source_target_pairs={{0,2},{2,4},{4,6},{6,8},{8,10},{10,12},{12,14},{14,16},{16,18},{18... | collective-permute-start | bytes 995336 | tf_op jit(solution)/shard_map/ppermute | solution.py:32
  137.8 9.4 %collective-permute-start.8 = (bf16[165888]{0:T(1024)(128)(2,1)S(1)}, bf16[165888]{0:T(1024)(128)(2,1)}, u32[]{:S(2)}, u32[]{:S(2)}) collective-permute-start(bf16[165888]{0:T(1024)(128)(2,1)S(1)} %collective-permute-done.7), channel_id=1, source_target_pairs={{0,2},{2,4},{4,6},{6,8},{8,10},{10,12},{12,14},{14,16},{16,18},{18... | collective-permute-start | bytes 995336 | tf_op jit(solution)/shard_map/ppermute | solution.py:32
  147.2 9.6 %collective-permute-start.9 = (bf16[165888]{0:T(1024)(128)(2,1)}, bf16[165888]{0:T(1024)(128)(2,1)}, u32[]{:S(2)}, u32[]{:S(2)}) collective-permute-start(bf16[165888]{0:T(1024)(128)(2,1)} %collective-permute-done.8), channel_id=1, source_target_pairs={{0,2},{2,4},{4,6},{6,8},{8,10},{10,12},{12,14},{14,16},{16,18},{18... | collective-permute-start | bytes 995336 | tf_op jit(solution)/shard_map/ppermute | solution.py:32
  156.7 9.6 %collective-permute-start.10 = (bf16[165888]{0:T(1024)(128)(2,1)}, bf16[165888]{0:T(1024)(128)(2,1)}, u32[]{:S(2)}, u32[]{:S(2)}) collective-permute-start(bf16[165888]{0:T(1024)(128)(2,1)} %collective-permute-done.9), channel_id=1, source_target_pairs={{0,2},{2,4},{4,6},{6,8},{8,10},{10,12},{12,14},{14,16},{16,18},{18... | collective-permute-start | bytes 995336 | tf_op jit(solution)/shard_map/ppermute | solution.py:32
  166.3 9.5 %collective-permute-start.11 = (bf16[165888]{0:T(1024)(128)(2,1)}, bf16[165888]{0:T(1024)(128)(2,1)S(1)}, u32[]{:S(2)}, u32[]{:S(2)}) collective-permute-start(bf16[165888]{0:T(1024)(128)(2,1)} %collective-permute-done.10), channel_id=1, source_target_pairs={{0,2},{2,4},{4,6},{6,8},{8,10},{10,12},{12,14},{14,16},{16,18},{18... | collective-permute-start | bytes 995336 | tf_op jit(solution)/shard_map/ppermute | solution.py:32
  175.7 9.3 %collective-permute-start.12 = (bf16[165888]{0:T(1024)(128)(2,1)S(1)}, bf16[165888]{0:T(1024)(128)(2,1)}, u32[]{:S(2)}, u32[]{:S(2)}) collective-permute-start(bf16[165888]{0:T(1024)(128)(2,1)S(1)} %collective-permute-done.11), channel_id=1, source_target_pairs={{0,2},{2,4},{4,6},{6,8},{8,10},{10,12},{12,14},{14,16},{16,18},{18... | collective-permute-start | bytes 995336 | tf_op jit(solution)/shard_map/ppermute | solution.py:32
  185.1 17.7 %collective-permute-start.13 = (bf16[165888]{0:T(1024)(128)(2,1)}, bf16[165888]{0:T(1024)(128)(2,1)}, u32[]{:S(2)}, u32[]{:S(2)}) collective-permute-start(bf16[165888]{0:T(1024)(128)(2,1)} %collective-permute-done.12), channel_id=1, source_target_pairs={{0,2},{2,4},{4,6},{6,8},{8,10},{10,12},{12,14},{14,16},{16,18},{18... | collective-permute-start | bytes 995336 | tf_op jit(solution)/shard_map/ppermute | solution.py:32
  202.8 74.7 %collective-permute-start.14 = (bf16[165888]{0:T(1024)(128)(2,1)}, bf16[165888]{0:T(1024)(128)(2,1)S(1)}, u32[]{:S(2)}, u32[]{:S(2)}) collective-permute-start(bf16[165888]{0:T(1024)(128)(2,1)} %collective-permute-done.13), channel_id=1, source_target_pairs={{0,2},{2,4},{4,6},{6,8},{8,10},{10,12},{12,14},{14,16},{16,18},{18... | collective-permute-start | bytes 995336 | tf_op jit(solution)/shard_map/ppermute | solution.py:32
  203.2 101.2 %copy-start.17 = (bf16[256,576]{0,1:T(8,128)(2,1)}, bf16[256,576]{0,1:T(8,128)(2,1)S(1)}, u32[]{:S(2)}) copy-start(bf16[256,576]{0,1:T(8,128)(2,1)S(1)} %multiply_convert_fusion.3) | copy-start | bytes 884740
  203.2 30.9 %copy-start.57 = (bf16[165888]{0:T(1024)(128)(2,1)S(1)}, bf16[165888]{0:T(1024)(128)(2,1)}, u32[]{:S(2)}) copy-start(bf16[165888]{0:T(1024)(128)(2,1)} %copy-done.56) | copy-start | bytes 995332
  227.8 31.1 %copy-start.59 = (bf16[165888]{0:T(1024)(128)(2,1)S(1)}, bf16[165888]{0:T(1024)(128)(2,1)}, u32[]{:S(2)}) copy-start(bf16[165888]{0:T(1024)(128)(2,1)} %copy-done.58) | copy-start | bytes 995332
  312.4 30.9 %copy-start.35 = (f32[256,64]{0,1:T(8,128)S(1)}, f32[256,64]{0,1:T(8,128)}, u32[]{:S(2)}) copy-start(f32[256,64]{0,1:T(8,128)} %copy-done.34) | copy-start | bytes 196612
  343.1 49.2 %reduce-scatter.5.cloned.1.call-start = ((), (), s32[]{:S(2)}) async-start(), calls=%async_computation.3 | async-start | bytes 589824 | tf_op jit(solution)/shard_map/reduce_scatter | solution.py:297
  372.7 304.0 %all-reduce.13.cloned.1.call-start = ((), (), s32[]{:S(2)}) async-start(), calls=%async_computation.6 | async-start | bytes 28327936
  425.6 277.7 %all-reduce.11.cloned.1.call-start = ((), (), s32[]{:S(2)}) async-start(), calls=%async_computation.5 | async-start | bytes 450560
  430.3 262.4 %copy-start.27 = (f32[165888]{0:T(1024)S(1)}, f32[165888]{0:T(1024)}, u32[]{:S(2)}) copy-start(f32[165888]{0:T(1024)} %param.21) | copy-start | bytes 1990660
  430.3 262.4 %copy-start.44 = (f32[165888]{0:T(1024)S(1)}, f32[165888]{0:T(1024)}, u32[]{:S(2)}) copy-start(f32[165888]{0:T(1024)} %param.22) | copy-start | bytes 1990660
  430.3 262.4 %copy-start.45 = (f32[165888]{0:T(1024)S(1)}, f32[165888]{0:T(1024)}, u32[]{:S(2)}) copy-start(f32[165888]{0:T(1024)} %param.23) | copy-start | bytes 1990660
  (62 other events, 419.9 us)
Sparse Core Ops, SparseCore 0:
  34.3 102.0 all-reduce.8
  343.2 14.3 reduce-scatter.2
  372.8 14.3 reduce-scatter.4
  425.7 250.9 all-reduce.12
  679.4 23.7 all-reduce.10
